TPU v7x, 256 devices: a whole 4x4x8 slice. The times are simulated.
256 devices in a mesh: dp: 8 (over z), seq: 32 (over x, y, core).
Axes of the slice: x: 4, y: 4, z: 8, core: 2. Of those that a mesh axis runs over, the one named last changes fastest.
Arguments:
- tokens: bfloat16 [128, 4, 2560], P('dp'), may hold values from -6 to 6
- attn_gain: float32 [2560], replicated, may hold values from 0.1 to 1.9
- qkv_weight: bfloat16 [3072, 2560], P(('seq', 'dp'))
- out_weight: bfloat16 [2560, 2560], P(('seq', 'dp')), may hold values from -0.125 to 0.125
- mlp_gain: float32 [2560], replicated, may hold values from 0.1 to 1.9
- gate_up: bfloat16 [2, 7680, 2560], P(None, 'seq'), may hold values from -0.125 to 0.125
- down_weight: bfloat16 [7680, 2560], P('seq'), may hold values from -0.0625 to 0.0625
- kv_pool: bfloat16 [4096, 128, 512], P(('dp', 'seq')), may hold values from -6 to 6
- cache_len: int32 [128], P('dp'), may hold values from 1 to 16384, as said below
- page_table: int32 [128, 16], P('dp'), may hold values from 0 to 511, as said below
Outputs:
- layer_out: bfloat16 [128, 4, 2560], P('dp')
- written_pool: bfloat16 [4096, 128, 512], P(('dp', 'seq'))
Inputs may be any that keep to these rules, and one draw needn't show every extreme that they name: `cache_len`: some request of the whole batch has exactly 16384 cached tokens; lengths under 2048 occur. `page_table`: within the 16 requests of one dp index all entries differ. Slot s lies on seq index s // 16; in every dp index some seq index holds exactly 16 of its pages.
All inputs are finite; a program needn't handle non-finite values.
Results may differ from a plain program's by a relative error of at most 0.018.
Values may be sent and summed in bfloat16 or wider, within the bound.
A program may use at most 128 MiB of HBM per device.

v0:
```python
import jax
import jax.numpy as jnp
from jax import lax
from jax.sharding import PartitionSpec as P

low_fill = -1e30


def rms_norm(values, gains):
    floats = values.astype(jnp.float32)
    return floats * lax.rsqrt(jnp.mean(floats * floats, axis=-1, keepdims=True) + 1e-06) * gains


def rotate(values, positions):
    quarter = values.shape[-1] // 4
    freq_index = jnp.arange(quarter).astype(jnp.float32)
    inverse = 10000.0 ** (-freq_index / quarter)
    angles = positions[..., None] * inverse
    first = values[..., :quarter]
    second = values[..., quarter : 2 * quarter]
    others = values[..., 2 * quarter :]
    cosine = jnp.cos(angles)
    sine = jnp.sin(angles)
    return jnp.concatenate(
        [first * cosine - second * sine, second * cosine + first * sine, others], axis=-1
    )


def body(
    tokens,
    attn_gain,
    qkv_weight,
    out_weight,
    mlp_gain,
    gate_up,
    down_weight,
    kv_pool,
    cache_len,
    page_table,
):
    seq_index = lax.axis_index("seq")
    requests, new_count, model_width = tokens.shape
    slot_count, page_len, pair_width = kv_pool.shape
    head_dim = pair_width // 2
    head_count = out_weight.shape[1] // head_dim
    page_count = page_table.shape[1]
    window = page_count * page_len
    row_count = requests * new_count
    query_rows = new_count * head_count
    split_q = head_count * head_dim
    scale = head_dim ** (-0.5)
    contract = (((1,), (1,)), ((), ()))
    qkv_local, out_local = (
        lax.all_gather(qkv_weight, "dp", axis=0, tiled=True),
        lax.all_gather(out_weight, "dp", axis=0, tiled=True),
    )
    normed = rms_norm(tokens, attn_gain).astype(jnp.bfloat16).reshape(row_count, model_width)
    local_part = lax.dot_general(
        normed, qkv_local, contract, preferred_element_type=jnp.float32
    ).astype(jnp.bfloat16)
    projected = lax.all_gather(local_part, "seq", axis=1, tiled=True).reshape(
        requests, new_count, -1
    )
    positions_int = cache_len[:, None] + jnp.arange(new_count, dtype=jnp.int32)[None, :]
    positions = positions_int.astype(jnp.float32)
    queries = rotate(
        projected[:, :, :split_q]
        .astype(jnp.float32)
        .reshape(requests, new_count, head_count, head_dim),
        positions[:, :, None],
    ).astype(jnp.bfloat16)
    keys_new = rotate(
        projected[:, :, split_q : split_q + head_dim].astype(jnp.float32), positions
    ).astype(jnp.bfloat16)
    values_new = projected[:, :, split_q + head_dim :]
    slot_ids = seq_index * slot_count + jnp.arange(slot_count, dtype=jnp.int32)
    matches = page_table[None, :, :] == slot_ids[:, None, None]
    owners = jnp.any(matches, axis=2)
    in_use = jnp.any(owners, axis=1)
    page_of = jnp.sum(
        jnp.where(matches, jnp.arange(page_count, dtype=jnp.int32)[None, None, :], 0), axis=(1, 2)
    )
    slot_length = jnp.sum(jnp.where(owners, cache_len[None, :], 0), axis=1)
    query_flat = queries.reshape(requests, query_rows * head_dim)
    slot_queries = jnp.dot(
        owners.astype(jnp.bfloat16), query_flat, preferred_element_type=jnp.float32
    )
    slot_queries = slot_queries.astype(jnp.bfloat16).reshape(slot_count, query_rows, head_dim)
    scores = (
        jnp.einsum(
            "pqd,pkd->pqk",
            slot_queries,
            kv_pool[:, :, :head_dim],
            preferred_element_type=jnp.float32,
        )
        * scale
    )
    cycle = page_of[:, None] * page_len + jnp.arange(page_len, dtype=jnp.int32)[None, :]
    key_pos = slot_length[:, None] - 1 - jnp.mod(slot_length[:, None] - 1 - cycle, window)
    query_pos = (
        slot_length[:, None] + (jnp.arange(query_rows, dtype=jnp.int32) // head_count)[None, :]
    )
    visible = (
        in_use[:, None, None]
        & (key_pos >= 0)[:, None, :]
        & (key_pos[:, None, :] > query_pos[:, :, None] - window)
    )
    slot_peak = jnp.max(jnp.where(visible, scores, low_fill), axis=2)
    weights = jnp.where(visible, jnp.exp(scores - slot_peak[:, :, None]), 0.0)
    slot_sum = jnp.sum(weights, axis=2)
    slot_out = jnp.einsum(
        "pqk,pkd->pqd",
        weights.astype(jnp.bfloat16),
        kv_pool[:, :, head_dim:],
        preferred_element_type=jnp.float32,
    )
    request_peak = jnp.max(jnp.where(owners[:, :, None], slot_peak[:, None, :], low_fill), axis=0)
    owner_peak = jnp.max(jnp.where(owners[:, :, None], request_peak[None, :, :], low_fill), axis=1)
    factor = jnp.exp(slot_peak - owner_peak)
    request_sum = jnp.sum(
        jnp.where(owners[:, :, None], (slot_sum * factor)[:, None, :], 0.0), axis=0
    )
    request_out = jnp.einsum(
        "pr,pqd->rqd",
        owners.astype(jnp.float32),
        slot_out * factor[:, :, None],
        precision=lax.Precision.HIGHEST,
    )
    query_block = queries.reshape(requests, query_rows, head_dim)
    new_scores = (
        jnp.einsum("rqd,rud->rqu", query_block, keys_new, preferred_element_type=jnp.float32)
        * scale
    )
    causal = jnp.arange(new_count)[None, :] <= (jnp.arange(query_rows) // head_count)[:, None]
    new_peak = jnp.max(jnp.where(causal[None], new_scores, low_fill), axis=2)
    global_peak = lax.pmax(request_peak, "seq")
    rescale = jnp.exp(request_peak - global_peak)
    old_denominator, weighted = (
        lax.psum((request_sum * rescale).astype(jnp.bfloat16), "seq").astype(jnp.float32),
        lax.psum((request_out * rescale[:, :, None]).astype(jnp.bfloat16), "seq").astype(
            jnp.float32
        ),
    )
    top_peak = jnp.maximum(global_peak, new_peak)
    new_weights = jnp.where(causal[None], jnp.exp(new_scores - top_peak[:, :, None]), 0.0)
    carried = jnp.exp(global_peak - top_peak)
    fresh_sum = jnp.sum(new_weights, axis=2)
    fresh_out = jnp.einsum(
        "rqu,rud->rqd",
        new_weights.astype(jnp.bfloat16),
        values_new,
        preferred_element_type=jnp.float32,
    )
    carried, fresh_sum, fresh_out = (carried, fresh_sum, fresh_out)
    denominator = old_denominator * carried + fresh_sum
    numerator = weighted * carried[:, :, None] + fresh_out
    attended = (
        (numerator / denominator[:, :, None]).astype(jnp.bfloat16).reshape(row_count, split_q)
    )
    heads_part = lax.dot_general(
        attended, out_local, contract, preferred_element_type=jnp.float32
    ).astype(jnp.bfloat16)
    heads_out = lax.all_gather(heads_part, "seq", axis=1, tiled=True)
    residual = (
        tokens.reshape(row_count, model_width).astype(jnp.float32) + heads_out.astype(jnp.float32)
    ).astype(jnp.bfloat16)
    hidden_in = rms_norm(residual, mlp_gain).astype(jnp.bfloat16)
    gate_and_up = jnp.einsum("rd,gfd->grf", hidden_in, gate_up, preferred_element_type=jnp.float32)
    hidden = (jax.nn.gelu(gate_and_up[0], approximate=True) * gate_and_up[1]).astype(jnp.bfloat16)
    partial_sum = jnp.dot(hidden, down_weight, preferred_element_type=jnp.float32)
    full_sum = lax.psum(partial_sum.astype(jnp.bfloat16), "seq").astype(jnp.float32)
    layer_out = (residual.astype(jnp.float32) + full_sum).astype(jnp.bfloat16)
    layer_out = layer_out.reshape(requests, new_count, model_width)
    page_index = jnp.mod(positions_int // page_len, page_count)
    slot_taken = jnp.take_along_axis(page_table, page_index, axis=1)
    local_slot = slot_taken - seq_index * slot_count
    local_slot = jnp.where((local_slot >= 0) & (local_slot < slot_count), local_slot, slot_count)
    offset = jnp.mod(positions_int, page_len)
    new_rows = jnp.concatenate([keys_new, values_new], axis=-1)
    written_pool = kv_pool.at[local_slot, offset].set(new_rows, mode="drop")
    return (layer_out, written_pool)


def solution(mesh):
    in_specs = (
        P("dp", None, None),
        P(),
        P(("seq", "dp"), None),
        P(("seq", "dp"), None),
        P(),
        P(None, "seq", None),
        P("seq", None),
        P(("dp", "seq"), None, None),
        P("dp"),
        P("dp", None),
    )
    out_specs = (P("dp", None, None), P(("dp", "seq"), None, None))
    return jax.shard_map(body, mesh=mesh, in_specs=in_specs, out_specs=out_specs, check_vma=False)
```

profile of v0, /device:TPU:1, one launch (start us, length us, event | category | flops | bytes accessed | tf_op | source)
XLA Modules:
  0.0 415.1 jit_solution(9135690108365068851)
XLA Ops:
  7.2 3.2 copy.131
  10.5 0.6 multiply_power_fusion
  11.1 24.0 %all-gather = bf16[8,12,2560]{2,1,0:T(8,128)(2,1)S(1)} all-gather(bf16[1,12,2560]{2,1,0:T(8,128)(2,1)S(1)} %bitcast.64), channel_id=1, replica_groups=mesh['dp'=8,'seq'=32] {'dp'}, dimensions={0}, use_global_device_ids=true | all-gather | bytes 552960 | tf_op jit(solution)/shard_map/all_gather | solution.py:54
  35.1 0.9 reshape.604
  36.0 0.3 multiply_reduce_fusion
  36.3 0.2 multiply_convert_fusion
  36.6 1.3 fusion.1
  37.9 31.8 %all-gather.1 = bf16[32,96,64]{1,2,0:T(8,128)(2,1)S(1)} all-gather(bf16[1,96,64]{1,2,0:T(8,128)(2,1)S(1)} %fusion.1), channel_id=1, replica_groups=mesh['dp'=8,'seq'=32] {'seq'}, dimensions={0}, use_global_device_ids=true | all-gather | bytes 405504 | tf_op jit(solution)/shard_map/all_gather | solution.py:61
  69.7 0.3 copy.91
  70.1 0.7 reshape.606
  70.8 0.2 reshape.581
  71.0 0.1 slice.62
  71.1 1.0 compare_reduce_fusion
  72.1 1.0 fusion.30
  73.1 0.5 and_select_fusion
  73.6 0.6 copy_convert_fusion.1
  74.3 0.5 add_convert_fusion.2
  74.8 0.9 copy_convert_fusion
  75.7 1.2 reshape.589
  77.0 1.0 subtract_convert_fusion.1
  78.1 0.2 subtract_convert_fusion
  78.4 0.3 pad_maximum_fusion
  78.7 0.4 copy-done.7
  79.2 0.9 convert_element_type.110
  80.1 0.1 select_reduce_fusion.5
  80.2 1.2 convolution_convert_fusion
  81.8 2.4 select_reduce_fusion
  84.3 0.1 select_reduce_fusion.3
  84.4 0.1 select_reduce_fusion.2
  84.5 63.2 %pmax.7 = f32[16,40]{1,0:T(8,128)S(1)} all-reduce(f32[16,40]{1,0:T(8,128)S(1)} %select_reduce_fusion.3), channel_id=1, replica_groups=mesh['dp'=8,'seq'=32] {'seq'}, use_global_device_ids=true, to_apply=%region_8.9 | all-reduce | flops 640 | bytes 5120 | tf_op jit(solution)/shard_map/pmax | solution.py:136
  147.9 1.5 fusion.22
  149.4 0.1 select_reduce_fusion.1
  149.7 0.6 convolution_multiply_fusion.1
  150.4 0.3 select_reduce_fusion.4
  150.7 0.7 copy.96
  151.4 2.1 fusion
  153.6 0.9 reshape.587
  154.4 0.7 shift-left_or_fusion
  155.2 65.4 %psum.22 = bf16[16,40]{1,0:T(8,128)(2,1)S(1)} all-reduce(bf16[16,40]{1,0:T(8,128)(2,1)S(1)} %get-tuple-element.8), channel_id=1, replica_groups=mesh['dp'=8,'seq'=32] {'seq'}, use_global_device_ids=true, to_apply=%region_13.14 | all-reduce | flops 640 | bytes 2560 | tf_op jit(solution)/shard_map/psum | solution.py:139
  220.6 0.6 fusion.52
  221.3 0.7 copy.106
  221.9 0.7 copy.108
  222.6 20.4 %all-gather.2 = bf16[8,10,2560]{2,1,0:T(8,128)(2,1)S(1)} all-gather(bf16[1,10,2560]{2,1,0:T(8,128)(2,1)} %bitcast.65), channel_id=1, replica_groups=mesh['dp'=8,'seq'=32] {'dp'}, dimensions={0}, use_global_device_ids=true | all-gather | bytes 460800 | tf_op jit(solution)/shard_map/all_gather | solution.py:55
  243.1 0.9 reshape.608
  244.1 0.6 reshape.598
  244.8 0.8 gather_fusion
  245.7 0.1 copy-done.12
  245.8 0.9 fusion.41
  246.7 16.8 %all-reduce.3.cloned.1.call-done = bf16[16,40,256]{2,0,1:T(8,128)(2,1)} async-done(((bf16[16,40,256]{2,0,1:T(8,128)(2,1)}), bf16[16,40,256]{2,0,1:T(8,128)(2,1)}) %all-reduce.3.cloned.1.call-update) | async-done | bytes 327696 | tf_op jit(solution)/shard_map/psum | solution.py:140
  263.5 1.3 fusion.11
  264.8 0.1 copy.109
  264.9 0.4 reshape.585
  265.3 1.3 fusion.2
  266.5 23.5 %all-gather.3 = bf16[32,80,64]{1,2,0:T(8,128)(2,1)S(1)} all-gather(bf16[1,80,64]{1,2,0:T(8,128)(2,1)S(1)} %fusion.2), channel_id=1, replica_groups=mesh['dp'=8,'seq'=32] {'seq'}, dimensions={0}, use_global_device_ids=true | all-gather | bytes 337920 | tf_op jit(solution)/shard_map/all_gather | solution.py:163
  290.1 0.3 copy.110
  290.4 1.4 reshape.611
  291.9 1.6 fusion.5
  293.5 0.9 convolution_bitcast_fusion
  294.4 1.1 convolution_convert_fusion.1
  295.5 0.1 fusion.59
  295.7 7.9 %scatter_fusion = bf16[16,128,512]{2,1,0:T(8,128)(2,1)} fusion(bf16[16,128,512]{2,1,0:T(8,128)(2,1)} %copy.131, s32[64]{0:T(128)S(1)} %reshape.596, bf16[64,512]{1,0:T(8,128)(2,1)S(1)} %copy-done.15), kind=kCustom, calls=%fused_computation.1 | custom fusion | bytes 197120 | tf_op jit(solution)/shard_map/scatter | solution.py:180
  303.6 102.8 %all-reduce.5.cloned.1.call-done = bf16[64,2560]{1,0:T(8,128)(2,1)} async-done(((bf16[64,2560]{1,0:T(8,128)(2,1)}), bf16[64,2560]{1,0:T(8,128)(2,1)}) %all-reduce.5.cloned.1.call-update) | async-done | bytes 327696 | tf_op jit(solution)/shard_map/psum | solution.py:171
  406.4 1.0 fusion.8
  407.5 0.8 reshape.586
  (92 shorter events, 1.5 us)
Async XLA Ops:
  7.2 286.3 %copy-start = (bf16[2,240,2560]{2,1,0:T(8,128)(2,1)S(1)}, bf16[2,240,2560]{2,1,0:T(8,128)(2,1)}, u32[]{:S(2)}) copy-start(bf16[2,240,2560]{2,1,0:T(8,128)(2,1)} %param.15) | copy-start | bytes 7372804
  7.2 28.8 %copy-start.3 = (bf16[16,4,2560]{2,1,0:T(4,128)(2,1)S(1)}, bf16[16,4,2560]{2,1,0:T(4,128)(2,1)}, u32[]{:S(2)}) copy-start(bf16[16,4,2560]{2,1,0:T(4,128)(2,1)} %param.10) | copy-start | bytes 983044
  7.2 3.9 copy-start.16
  7.2 256.3 %all-reduce.3.cloned.1.call-start = ((), (), s32[]{:S(2)}) async-start(), calls=%async_computation | async-start | bytes 655360 | tf_op jit(solution)/shard_map/psum | solution.py:140
  10.5 25.8 %copy-start.22 = (f32[2560]{0:T(1024)S(1)}, f32[2560]{0:T(1024)}, u32[]{:S(2)}) copy-start(f32[2560]{0:T(1024)} %param.11) | copy-start | bytes 30724
  37.9 33.2 %copy-start.1 = (s32[16,16]{1,0:T(8,128)S(1)}, s32[16,16]{1,0:T(8,128)}, u32[]{:S(2)}) copy-start(s32[16,16]{1,0:T(8,128)} %param.19) | copy-start | bytes 3076
  37.9 36.3 %copy-start.23 = (s32[16]{0:T(128)S(1)}, s32[16]{0:T(128)}, u32[]{:S(2)}) copy-start(s32[16]{0:T(128)} %param.18) | copy-start | bytes 196
  70.9 3.9 copy-start.11
  77.0 1.3 copy-start.5
  78.3 0.7 copy-start.7
  78.3 0.8 copy-start.9
  78.4 3.2 copy-start.27
  78.4 3.3 copy-start.26
  78.4 3.4 copy-start.28
  79.2 68.5 %copy-start.10 = (bf16[16,4,10,64]{3,2,0,1:T(8,128)(2,1)S(1)}, bf16[16,4,10,64]{3,2,0,1:T(8,128)(2,1)}, u32[]{:S(2)}) copy-start(bf16[16,4,10,64]{3,2,0,1:T(8,128)(2,1)} %copy-done.9) | copy-start | bytes 245764
  80.1 67.6 %copy-start.8 = (bf16[16,4,10,64]{3,2,0,1:T(8,128)(2,1)S(1)}, bf16[16,4,10,64]{3,2,0,1:T(8,128)(2,1)}, u32[]{:S(2)}) copy-start(bf16[16,4,10,64]{3,2,0,1:T(8,128)(2,1)} %copy-done.7) | copy-start | bytes 245764
  80.2 67.6 %copy-start.6 = (bf16[16,4,10,128]{3,2,0,1:T(8,128)(2,1)S(1)}, bf16[16,4,10,128]{3,2,0,1:T(8,128)(2,1)}, u32[]{:S(2)}) copy-start(bf16[16,4,10,128]{3,2,0,1:T(8,128)(2,1)} %copy-done.5) | copy-start | bytes 491524
  147.7 2.0 copy-start.2
  147.7 2.0 copy-start.13
  147.8 2.6 slice-start
  147.9 2.8 copy-start.25
  149.6 1.1 copy-start.17
  149.6 1.1 copy-start.19
  149.7 3.8 copy-start.4
  151.4 92.6 %slice-start.1 = ((bf16[16,4,3072]{2,1,0:T(4,128)(2,1)}), bf16[16,4,384]{2,1,0:T(4,128)(2,1)S(1)}, s32[]{:S(2)}) async-start(bf16[16,4,3072]{2,1,0:T(4,128)(2,1)} %copy-done.11), calls=%async_computation.3 | async-start | bytes 98304 | tf_op jit(solution)/shard_map/slice | solution.py:21
  153.5 90.5 %copy-start.18 = (bf16[16,4,64]{2,1,0:T(4,128)(2,1)S(1)}, bf16[16,4,64]{2,1,0:T(4,128)(2,1)}, u32[]{:S(2)}) copy-start(bf16[16,4,64]{2,1,0:T(4,128)(2,1)} %copy-done.17) | copy-start | bytes 24580
  153.5 90.5 %copy-start.20 = (bf16[16,4,64]{2,1,0:T(4,128)(2,1)S(1)}, bf16[16,4,64]{2,1,0:T(4,128)(2,1)}, u32[]{:S(2)}) copy-start(bf16[16,4,64]{2,1,0:T(4,128)(2,1)} %copy-done.19) | copy-start | bytes 24580
  153.5 252.9 %all-reduce.5.cloned.1.call-start = ((), (), s32[]{:S(2)}) async-start(), calls=%async_computation.1 | async-start | bytes 655360 | tf_op jit(solution)/shard_map/psum | solution.py:171
  244.8 1.0 copy-start.12
  290.1 3.4 copy-start.21
  291.9 2.5 copy-start.14
  293.5 2.0 copy-start.24
  293.5 2.2 copy-start.15
Sparse Core Ops, SparseCore 0:
  153.6 109.8 all-reduce.2
  295.6 110.8 all-reduce.4
where the time goes:
time: 416 us; the launch traced here: 415 us
  blocking collectives  228 us (55%)
  waiting for transfers between devices  120 us (29%)
  local copies, waits for them, and re-layouts  25.4 us (6%)
  other arithmetic  14.8 us (4%)
  between operations  14.7 us (4%)
  matrix products  12 us (3%)
    psum x1, waiting for transfers between devices, body(): lax.psum(partial_sum.astype(jnp.bfloat16), 'seq').astype(jnp.float32)  103 us
    psum x1, blocking collectives, body(): lax.psum((request_sum * rescale).astype(jnp.bfloat16), 'seq')  65.4 us
    pmax x1, blocking collectives, body(): global_peak = lax.pmax(request_peak, 'seq')  63.2 us
    all_gather x1, blocking collectives, body(): lax.all_gather(local_part, 'seq', axis=1, tiled=True)  31.8 us
    all_gather x1, blocking collectives, body(): lax.all_gather(qkv_weight, 'dp', axis=0, tiled=True)  24 us
    all_gather x1, blocking collectives, body(): heads_out = lax.all_gather(heads_part, 'seq', axis=1, tiled=True)  23.5 us
    all_gather x1, blocking collectives, body(): lax.all_gather(out_weight, 'dp', axis=0, tiled=True)  20.4 us
    psum x1, waiting for transfers between devices, body(): lax.psum((request_out * rescale[:, :, None]).astype(jnp.bfloat16), 'seq')  16.8 us
  transfers between devices with their start and end apart: 2, of which 2 were waited for; matrix products, arithmetic and copies ran while one was open for 4% of the time, Pallas kernels for 0%

commit v1 on v0

--- a/solution.py
+++ b/solution.py
@@ -168,7 +168,9 @@
     gate_and_up = jnp.einsum("rd,gfd->grf", hidden_in, gate_up, preferred_element_type=jnp.float32)
     hidden = (jax.nn.gelu(gate_and_up[0], approximate=True) * gate_and_up[1]).astype(jnp.bfloat16)
     partial_sum = jnp.dot(hidden, down_weight, preferred_element_type=jnp.float32)
-    full_sum = lax.psum(partial_sum.astype(jnp.bfloat16), "seq").astype(jnp.float32)
+    full_sum = jnp.sum(lax.all_gather(partial_sum.astype(jnp.bfloat16), "seq"), axis=0).astype(
+        jnp.float32
+    )
     layer_out = (residual.astype(jnp.float32) + full_sum).astype(jnp.bfloat16)
     layer_out = layer_out.reshape(requests, new_count, model_width)
     page_index = jnp.mod(positions_int // page_len, page_count)

time: 416 us -> 371 us (0.89)
  waiting for transfers between devices: 120 us -> 64.9 us
  blocking collectives: 228 us -> 234 us
  other arithmetic: 14.8 us -> 19.3 us
    psum x1 -> x0, waiting for transfers between devices: 103 us -> none  [body(): lax.psum(partial_sum.astype(jnp.bfloat16), 'seq').astype(jnp.float32)]
    all_gather x0 -> x1, waiting for transfers between devices: none -> 51.9 us  [body(): lax.all_gather(partial_sum.astype(jnp.bfloat16), 'seq')]
    reduce_sum x0 -> x1, other arithmetic: none -> 5.69 us  [body(): jnp.sum(lax.all_gather(partial_sum.astype(jnp.bfloat16), 'seq'), axis=0)]
    psum x1, blocking collectives: 65.4 us -> 70.6 us  [body(): lax.psum((request_sum * rescale).astype(jnp.bfloat16), 'seq')]
where the time goes in v1:
time: 371 us; the launch traced here: 370 us
  blocking collectives  234 us (63%)
  waiting for transfers between devices  64.9 us (17%)
  local copies, waits for them, and re-layouts  25.5 us (7%)
  other arithmetic  19.3 us (5%)
  between operations  14.7 us (4%)
  matrix products  11.9 us (3%)
    psum x1, blocking collectives, body(): lax.psum((request_sum * rescale).astype(jnp.bfloat16), 'seq')  70.6 us
    pmax x1, blocking collectives, body(): global_peak = lax.pmax(request_peak, 'seq')  63.2 us
    all_gather x1, waiting for transfers between devices, body(): lax.all_gather(partial_sum.astype(jnp.bfloat16), 'seq')  51.9 us
    all_gather x1, blocking collectives, body(): lax.all_gather(local_part, 'seq', axis=1, tiled=True)  31.8 us
    all_gather x1, blocking collectives, body(): lax.all_gather(qkv_weight, 'dp', axis=0, tiled=True)  24 us
    all_gather x1, blocking collectives, body(): heads_out = lax.all_gather(heads_part, 'seq', axis=1, tiled=True)  23.5 us
    all_gather x1, blocking collectives, body(): lax.all_gather(out_weight, 'dp', axis=0, tiled=True)  20.7 us
    psum x1, waiting for transfers between devices, body(): lax.psum((request_out * rescale[:, :, None]).astype(jnp.bfloat16), 'seq')  13 us
  transfers between devices with their start and end apart: 2, of which 2 were waited for; matrix products, arithmetic and copies ran while one was open for 4% of the time, Pallas kernels for 0%

profile of v1, /device:TPU:1, one launch (start us, length us, event | category | flops | bytes accessed | tf_op | source)
XLA Modules:
  0.0 370.2 jit_solution(3798607268583272912)
XLA Ops:
  7.3 3.2 copy.130
  10.5 0.6 and_select_fusion
  11.1 0.5 multiply_power_fusion
  11.6 0.4 fusion.30
  12.1 1.0 compare_reduce_fusion
  13.1 0.3 multiply_reduce_fusion
  13.3 0.2 multiply_convert_fusion
  13.7 24.0 %all-gather.1 = bf16[8,12,2560]{2,1,0:T(8,128)(2,1)S(1)} all-gather(bf16[1,12,2560]{2,1,0:T(8,128)(2,1)S(1)} %bitcast.67), channel_id=1, replica_groups=mesh['dp'=8,'seq'=32] {'dp'}, dimensions={0}, use_global_device_ids=true | all-gather | bytes 552960 | tf_op jit(solution)/shard_map/all_gather | solution.py:54
  37.7 0.9 reshape.605
  38.6 1.3 fusion.1
  39.9 31.8 %all-gather.2 = bf16[32,96,64]{1,2,0:T(8,128)(2,1)S(1)} all-gather(bf16[1,96,64]{1,2,0:T(8,128)(2,1)S(1)} %fusion.1), channel_id=1, replica_groups=mesh['dp'=8,'seq'=32] {'seq'}, dimensions={0}, use_global_device_ids=true | all-gather | bytes 405504 | tf_op jit(solution)/shard_map/all_gather | solution.py:61
  71.7 0.3 copy.91
  72.0 0.7 reshape.607
  72.8 0.2 reshape.581
  73.0 0.1 slice.62
  73.1 0.6 copy_convert_fusion.1
  73.7 0.9 copy_convert_fusion
  74.6 1.2 reshape.589
  76.0 1.6 subtract_convert_fusion.1
  77.6 0.2 subtract_convert_fusion
  77.8 0.7 copy.97
  78.6 0.3 pad_maximum_fusion
  78.9 0.7 copy.99
  79.6 0.6 iota_compare_fusion
  80.2 0.1 select_reduce_fusion.5
  80.6 0.2 convert_element_type.112
  80.8 0.2 convolution_convert_fusion
  81.1 1.8 select_reduce_fusion
  82.9 0.1 select_reduce_fusion.3
  83.0 63.2 %pmax.7 = f32[16,40]{1,0:T(8,128)S(1)} all-reduce(f32[16,40]{1,0:T(8,128)S(1)} %select_reduce_fusion.3), channel_id=1, replica_groups=mesh['dp'=8,'seq'=32] {'seq'}, use_global_device_ids=true, to_apply=%region_8.9 | all-reduce | flops 640 | bytes 5120 | tf_op jit(solution)/shard_map/pmax | solution.py:136
  146.2 0.1 select_reduce_fusion.2
  146.3 0.7 copy.104
  147.3 0.4 fusion.22
  147.7 0.1 select_reduce_fusion.1
  147.8 1.6 select_reduce_fusion.4
  149.4 0.6 multiply_convert_fusion.1
  150.0 0.7 copy.96
  150.7 1.7 convolution_multiply_fusion.1
  152.4 2.1 fusion
  154.6 0.9 reshape.587
  155.5 20.7 %all-gather.3 = bf16[8,10,2560]{2,1,0:T(8,128)(2,1)S(1)} all-gather(bf16[1,10,2560]{2,1,0:T(8,128)(2,1)} %bitcast.68), channel_id=1, replica_groups=mesh['dp'=8,'seq'=32] {'dp'}, dimensions={0}, use_global_device_ids=true | all-gather | bytes 460800 | tf_op jit(solution)/shard_map/all_gather | solution.py:55
  176.2 0.9 reshape.609
  177.1 70.6 %psum.15 = bf16[16,40]{1,0:T(8,128)(2,1)S(1)} all-reduce(bf16[16,40]{1,0:T(8,128)(2,1)} %get-tuple-element.8), channel_id=1, replica_groups=mesh['dp'=8,'seq'=32] {'seq'}, use_global_device_ids=true, to_apply=%region_13.14 | all-reduce | flops 640 | bytes 2560 | tf_op jit(solution)/shard_map/psum | solution.py:139
  247.7 0.7 fusion.52
  248.4 0.7 multiply_add_fusion
  249.1 0.7 copy.108
  249.8 0.7 copy.106
  250.5 1.0 fusion.41
  251.5 13.0 %all-reduce.2.cloned.1.call-done = bf16[16,40,256]{2,0,1:T(8,128)(2,1)} async-done(((bf16[16,40,256]{2,0,1:T(8,128)(2,1)}), bf16[16,40,256]{2,0,1:T(8,128)(2,1)}) %all-reduce.2.cloned.1.call-update) | async-done | bytes 327696 | tf_op jit(solution)/shard_map/psum | solution.py:140
  264.5 1.3 fusion.11
  265.9 0.4 reshape.585
  266.3 0.3 fusion.2
  266.6 23.5 %all-gather.4 = bf16[32,80,64]{1,2,0:T(8,128)(2,1)S(1)} all-gather(bf16[1,80,64]{1,2,0:T(8,128)(2,1)S(1)} %fusion.2), channel_id=1, replica_groups=mesh['dp'=8,'seq'=32] {'seq'}, dimensions={0}, use_global_device_ids=true | all-gather | bytes 337920 | tf_op jit(solution)/shard_map/all_gather | solution.py:163
  290.1 0.3 copy.110
  290.4 1.4 reshape.612
  291.9 1.6 fusion.5
  293.5 0.9 convolution_bitcast_fusion
  294.4 1.1 convolution_convert_fusion.1
  295.7 0.8 gather_fusion
  296.6 0.1 fusion.59
  296.9 7.9 %scatter_fusion = bf16[16,128,512]{2,1,0:T(8,128)(2,1)} fusion(bf16[16,128,512]{2,1,0:T(8,128)(2,1)} %copy.130, s32[64]{0:T(128)S(1)} %reshape.596, bf16[64,512]{1,0:T(8,128)(2,1)S(1)} %reshape.598), kind=kCustom, calls=%fused_computation.1 | custom fusion | bytes 197120 | tf_op jit(solution)/shard_map/scatter | solution.py:182
  304.9 51.9 %all-gather.7.cloned.1.call-done = bf16[2048,2560]{1,0:T(8,128)(2,1)} async-done(((bf16[64,2560]{1,0:T(8,128)(2,1)}), bf16[2048,2560]{1,0:T(8,128)(2,1)}) %all-gather.7.cloned.1.call-update) | async-done | bytes 10485776 | tf_op jit(solution)/shard_map/all_gather | solution.py:171
  356.7 5.7 %reduce_sum.82 = bf16[64,2560]{1,0:T(8,128)(2,1)S(1)} reduce(bf16[32,64,2560]{2,1,0:T(8,128)(2,1)} %bitcast.60, bf16[]{:T(256)} %constant.120.clone.1), dimensions={0}, to_apply=%region_16.17 | reduce | flops 5079040 | bytes 10813442 | tf_op jit(solution)/shard_map/reduce_sum | solution.py:171
  362.5 0.8 reshape.586
  (85 shorter events, 1.6 us)
Async XLA Ops:
  7.2 286.3 %copy-start = (bf16[2,240,2560]{2,1,0:T(8,128)(2,1)S(1)}, bf16[2,240,2560]{2,1,0:T(8,128)(2,1)}, u32[]{:S(2)}) copy-start(bf16[2,240,2560]{2,1,0:T(8,128)(2,1)} %param.15) | copy-start | bytes 7372804
  7.2 5.9 %copy-start.2 = (bf16[16,4,2560]{2,1,0:T(4,128)(2,1)S(1)}, bf16[16,4,2560]{2,1,0:T(4,128)(2,1)}, u32[]{:S(2)}) copy-start(bf16[16,4,2560]{2,1,0:T(4,128)(2,1)} %param.10) | copy-start | bytes 983044
  7.2 6.1 %copy-start.19 = (f32[2560]{0:T(1024)S(1)}, f32[2560]{0:T(1024)}, u32[]{:S(2)}) copy-start(f32[2560]{0:T(1024)} %param.11) | copy-start | bytes 30724
  7.2 6.5 %copy-start.12 = (bf16[12,2560]{1,0:T(8,128)(2,1)S(1)}, bf16[12,2560]{1,0:T(8,128)(2,1)}, u32[]{:S(2)}) copy-start(bf16[12,2560]{1,0:T(8,128)(2,1)} %param.12) | copy-start | bytes 184324
  7.2 4.4 %copy-start.1 = (s32[16,16]{1,0:T(8,128)S(1)}, s32[16,16]{1,0:T(8,128)}, u32[]{:S(2)}) copy-start(s32[16,16]{1,0:T(8,128)} %param.19) | copy-start | bytes 3076
  7.2 257.3 %all-reduce.2.cloned.1.call-start = ((), (), s32[]{:S(2)}) async-start(), calls=%async_computation | async-start | bytes 655360 | tf_op jit(solution)/shard_map/psum | solution.py:140
  13.1 134.6 %copy-start.11 = (pred[16,16]{1,0:T(8,128)(4,1)}, pred[16,16]{1,0:T(8,128)(4,1)S(1)}, u32[]{:S(2)}) copy-start(pred[16,16]{1,0:T(8,128)(4,1)S(1)} %get-tuple-element.3) | copy-start | bytes 772
  39.9 33.2 %copy-start.20 = (s32[16]{0:T(128)S(1)}, s32[16]{0:T(128)}, u32[]{:S(2)}) copy-start(s32[16]{0:T(128)} %param.18) | copy-start | bytes 196
  72.9 0.8 copy-start.4
  72.9 3.0 copy-start.23
  77.6 2.0 copy-start.24
  77.6 2.8 copy-start.22
  80.8 66.3 %copy-start.8 = (bf16[16,4,10,64]{3,0,2,1:T(8,128)(2,1)S(1)}, bf16[16,4,10,64]{3,0,2,1:T(8,128)(2,1)}, u32[]{:S(2)}) copy-start(bf16[16,4,10,64]{3,0,2,1:T(8,128)(2,1)} %copy.97) | copy-start | bytes 245764
  80.8 66.3 %copy-start.9 = (bf16[16,4,10,128]{3,0,2,1:T(8,128)(2,1)S(1)}, bf16[16,4,10,128]{3,0,2,1:T(8,128)(2,1)}, u32[]{:S(2)}) copy-start(bf16[16,4,10,128]{3,0,2,1:T(8,128)(2,1)} %copy.99) | copy-start | bytes 491524
  81.1 66.7 %slice-start = ((bf16[16,4,3072]{2,1,0:T(4,128)(2,1)}), bf16[16,4,128]{2,1,0:T(4,128)(2,1)S(1)}, s32[]{:S(2)}) async-start(bf16[16,4,3072]{2,1,0:T(4,128)(2,1)} %copy-done.4), calls=%async_computation.2 | async-start | bytes 32768 | tf_op jit(solution)/shard_map/slice | solution.py:21
  146.2 4.5 %copy-start.13 = (f32[16,40]{1,0:T(8,128)}, f32[16,40]{1,0:T(8,128)S(1)}, u32[]{:S(2)}) copy-start(f32[16,40]{1,0:T(8,128)S(1)} %pmax.7) | copy-start | bytes 7684
  147.1 3.6 copy-start.14
  147.1 3.0 copy-start.16
  147.8 6.8 %copy-start.3 = (bf16[16,4,2560]{2,1,0:T(4,128)(2,1)S(1)}, bf16[16,4,2560]{2,1,0:T(4,128)(2,1)}, u32[]{:S(2)}) copy-start(bf16[16,4,2560]{2,1,0:T(4,128)(2,1)} %param.10) | copy-start | bytes 983044
  152.4 95.3 %copy-start.10 = (f32[16,40,4]{1,2,0:T(4,128)S(1)}, f32[16,40,4]{1,2,0:T(4,128)}, u32[]{:S(2)}) copy-start(f32[16,40,4]{1,2,0:T(4,128)} %get-tuple-element.22) | copy-start | bytes 30724
  152.4 98.1 %copy-start.5 = (bf16[16,4,3072]{2,1,0:T(4,128)(2,1)S(1)}, bf16[16,4,3072]{2,1,0:T(4,128)(2,1)}, u32[]{:S(2)}) copy-start(bf16[16,4,3072]{2,1,0:T(4,128)(2,1)} %copy-done.4) | copy-start | bytes 1179652
  154.5 202.2 %all-gather.7.cloned.1.call-start = ((), (), s32[]{:S(2)}) async-start(), calls=%async_computation.1 | async-start | bytes 10813440 | tf_op jit(solution)/shard_map/all_gather | solution.py:171
  251.5 14.8 %copy-start.6 = (bf16[80,2560]{1,0:T(8,128)(2,1)S(1)}, bf16[80,2560]{1,0:T(8,128)(2,1)}, u32[]{:S(2)}) copy-start(bf16[80,2560]{1,0:T(8,128)(2,1)} %reshape.609) | copy-start | bytes 1228804
  290.1 3.4 copy-start.18
  291.9 2.5 copy-start.7
  293.5 2.0 copy-start.21
  295.7 1.1 slice-start.1
  295.7 1.1 copy-start.15
  295.7 1.1 copy-start.17
Sparse Core Ops, SparseCore 0:
  154.6 109.8 all-reduce.1
  295.6 61.1 all-gather.6
